TPU v7x, 32 devices: a whole 2x2x4 slice. The times are simulated.
32 devices in a mesh: seq: 16 (over z, y, x), tp: 2 (over core).
Axes of the slice: x: 2, y: 2, z: 4, core: 2. Of those that a mesh axis runs over, the one named last changes fastest.
Arguments:
- tokens: bfloat16 [2048, 2048], P('seq'), may hold values from -6 to 6
- attn_gain: float32 [2048], replicated, may hold values from 0.1 to 1.9
- mlp_gain: float32 [2048], replicated, may hold values from 0.1 to 1.9
- w_query: float32 [2048, 2048], P('seq', 'tp'), may hold values from -0.70710678 to 0.70710678
- w_key: float32 [2048, 2048], P('seq', 'tp'), may hold values from -0.70710678 to 0.70710678
- w_value: float32 [2048, 2048], P('seq', 'tp'), may hold values from -0.125 to 0.125
- w_out: float32 [2048, 2048], P('tp', 'seq'), may hold values from -0.125 to 0.125
- sink_logits: float32 [16], P('tp'), may hold values from 8 to 16
- router: float32 [2048, 16], P('seq'), may hold values from -0.25 to 0.25
- expert_gate: float32 [16, 2048, 1024], P(None, 'seq', 'tp'), may hold values from -0.125 to 0.125
- expert_up: float32 [16, 2048, 1024], P(None, 'seq', 'tp'), may hold values from -0.125 to 0.125
- expert_down: float32 [16, 2048, 1024], P(None, 'seq', 'tp'), may hold values from -0.1875 to 0.1875
- layout_map: int32 [16], replicated, may hold values from 0 to 15, each once
- real_lengths: int32 [2], replicated, may hold values from 256 to 1088, as said below
- routes: int32 [2048, 8], P('seq'), may hold values from 0 to 15, all different within a row; in each aligned block of 128 rows (0 to 127, 128 to 255, ...) at most 72 rows name the same one
Outputs:
- layer_out: bfloat16 [2048, 2048], P('seq', 'tp')
Inputs may be any that keep to these rules, and one draw needn't show every extreme that they name: Prompt p has real tokens in the first real_lengths[p] of its slots and padding after them; each length is at least 256; the last prompt has no padding. `routes`: each row names 8 different experts; among the rows of one device no expert is named more than 72 times, and in some device some expert exactly 72 times. `layout_map`: each trainer expert is held by exactly one server expert number.
All inputs are finite; a program needn't handle non-finite values.
Results may differ from a plain program's by a relative error of at most 0.0075.
The roundings to bfloat16 on the way count: a program that leaves them out, or rounds other values in their place, can miss the bound.
Values may be sent and summed in bfloat16 or wider, within the bound.
No kernel may reach another device: no remote copies, remote signals or barrier semaphores. Data moves between devices by JAX's collectives and lax.ppermute only.
A program may use at most 128 MiB of HBM per device.

v0:
```python
import jax
import jax.numpy as jnp
from jax import lax
from jax.sharding import PartitionSpec as P

HEAD = 128
HALF_WIN = 2048
EPSILON = 1e-05
ROPE_BASE = 50000.0
MASKED = -1e30


def from_behind(value, axis, steps):
    count = lax.axis_size(axis)
    first, last = (max(0, -steps), min(count, count - steps))
    return lax.ppermute(value, axis, [(source, source + steps) for source in range(first, last)])


def rms_scale(row_values, gain_vector):
    mean_square = jnp.mean(row_values * row_values, axis=-1, keepdims=True)
    return row_values * lax.rsqrt(mean_square + EPSILON) * gain_vector


def rotate(head_block, positions):
    half_dim = head_block.shape[-1] // 2
    frequency = ROPE_BASE ** (-jnp.arange(half_dim, dtype=jnp.float32) / half_dim)
    angles = positions[:, None, None] * frequency[None, None, :]
    cosine = jnp.cos(angles)
    sine_part = jnp.sin(angles)
    first_half = head_block[..., :half_dim]
    second_half = head_block[..., half_dim:]
    return jnp.concatenate(
        [
            first_half * cosine - second_half * sine_part,
            second_half * cosine + first_half * sine_part,
        ],
        axis=-1,
    )


def length_of(prompt, real_lengths):
    one_hot = prompt[:, None] == jnp.arange(real_lengths.shape[0], dtype=jnp.int32)[None, :]
    return jnp.sum(jnp.where(one_hot, real_lengths[None, :], 0), axis=1)


def prompt_split(slot_ids, slot_len, stagger, prompt_count):
    prompt = jnp.minimum((slot_ids + stagger) // slot_len, prompt_count - 1)
    start = jnp.maximum(prompt * slot_len - stagger, 0)
    return (prompt, slot_ids - start)


def key_rules(query_ids, key_ids, slot_len, stagger, total_slots, real_lengths):
    prompt_count = real_lengths.shape[0]
    key_prompt, key_pos = prompt_split(key_ids, slot_len, stagger, prompt_count)
    query_prompt = prompt_split(query_ids, slot_len, stagger, prompt_count)[0]
    inside = (key_ids >= 0) & (key_ids < total_slots)
    key_live = inside & (key_pos < length_of(key_prompt, real_lengths))
    same_prompt = query_prompt[:, None] == key_prompt[None, :]
    nearby = jnp.abs(query_ids[:, None] - key_ids[None, :]) < HALF_WIN
    return same_prompt & nearby & key_live[None, :]


def attend(softmax_state, query_rows, key_rows, value_rows, allowed):
    running_max, denominator, accumulated = softmax_state
    scores = jnp.einsum(
        "tge,kge->gtk", query_rows, key_rows, preferred_element_type=jnp.float32
    ) * HEAD ** (-0.5)
    scores = jnp.where(allowed[None], scores, MASKED)
    new_max = jnp.maximum(running_max, jnp.max(scores, axis=2))
    rescale = jnp.exp(running_max - new_max)
    weight_tensors = jnp.exp(scores - new_max[:, :, None])
    denominator = denominator * rescale + jnp.sum(weight_tensors, axis=2)
    accumulated = accumulated * rescale[:, :, None] + jnp.einsum(
        "ytz,zyb->ytb",
        weight_tensors,
        value_rows.astype(jnp.float32),
        precision=lax.Precision.HIGHEST,
    )
    return (new_max, denominator, accumulated)


def shards(
    tokens,
    attn_gain,
    mlp_gain,
    w_query,
    w_key,
    w_value,
    w_out,
    sink_logits,
    router,
    expert_gate,
    expert_up,
    expert_down,
    layout_map,
    real_lengths,
    routes,
):
    token_count, model_width = tokens.shape
    seq_count = lax.axis_size("seq")
    tp_count = lax.axis_size("tp")
    expert_count = router.shape[1]
    route_count = routes.shape[1]
    head_count = sink_logits.shape[0]
    proj_width = head_count * HEAD
    col_share = model_width // tp_count
    total_slots = token_count * seq_count
    prompt_count = real_lengths.shape[0]
    slot_len = total_slots // prompt_count
    stagger = token_count // 2
    capacity = max(2, min(token_count, 9 * token_count * route_count // (8 * expert_count)))
    seq_place = lax.axis_index("seq")
    tp_place = lax.axis_index("tp")
    offsets = jnp.arange(token_count, dtype=jnp.int32)
    token_index = seq_place * token_count + offsets
    prompt, position = prompt_split(token_index, slot_len, stagger, prompt_count)
    valid_token = position < length_of(prompt, real_lengths)
    normed = rms_scale(tokens.astype(jnp.float32), attn_gain).astype(jnp.bfloat16)
    stack_local = jnp.concatenate([w_query, w_key, w_value], axis=1).astype(jnp.bfloat16)
    router_local = router.astype(jnp.bfloat16)
    stack_piece = lax.all_gather(stack_local, "seq", axis=0, tiled=True)
    router_piece = lax.all_gather(router_local, "seq", axis=0, tiled=True)
    product = jnp.dot(normed, stack_piece, preferred_element_type=jnp.float32)
    router_full = router_piece
    product, router_full = (product, router_full)
    rotary_positions = position.astype(jnp.float32)
    query_rows = rotate(
        product[:, :proj_width].reshape(token_count, head_count, HEAD), rotary_positions
    ).astype(jnp.bfloat16)
    key_rows = rotate(
        product[:, proj_width : 2 * proj_width].reshape(token_count, head_count, HEAD),
        rotary_positions,
    ).astype(jnp.bfloat16)
    value_rows = (
        product[:, 2 * proj_width :].astype(jnp.bfloat16).reshape(token_count, head_count, HEAD)
    )
    softmax_state = (
        jnp.broadcast_to(sink_logits[:, None], (head_count, token_count)),
        jnp.ones((head_count, token_count), jnp.float32),
        jnp.zeros((head_count, token_count, HEAD), jnp.float32),
    )
    softmax_state = attend(
        softmax_state,
        query_rows,
        key_rows,
        value_rows,
        key_rules(token_index, token_index, slot_len, stagger, total_slots, real_lengths),
    )
    own_pair = jnp.stack([key_rows, value_rows])

    def one_turn(turn_index, loop_carry):
        loop_state, from_below, from_above = loop_carry
        from_below = from_behind(from_below, "seq", 1)
        from_above = from_behind(from_above, "seq", -1)
        reach_rows = (turn_index + 1) * token_count
        key_ids = jnp.concatenate([token_index - reach_rows, token_index + reach_rows])
        neighbours = jnp.concatenate([from_below, from_above], axis=1)
        allowed = key_rules(token_index, key_ids, slot_len, stagger, total_slots, real_lengths)
        loop_state = attend(loop_state, query_rows, neighbours[0], neighbours[1], allowed)
        return (loop_state, from_below, from_above)

    softmax_state, from_below, from_above = lax.fori_loop(
        0, HALF_WIN // token_count, one_turn, (softmax_state, own_pair, own_pair)
    )
    running_max, denominator, accumulated = softmax_state
    attention_result = (
        jnp.transpose(accumulated / denominator[:, :, None], (1, 0, 2))
        .reshape(token_count, proj_width)
        .astype(jnp.bfloat16)
    )
    partial_out = jnp.dot(
        attention_result,
        lax.all_gather(w_out.astype(jnp.bfloat16), "seq", axis=1, tiled=True),
        preferred_element_type=jnp.float32,
    )
    mixed_full = lax.psum(partial_out, "tp")
    full_rows = tokens.astype(jnp.float32) + mixed_full
    outgoing = rms_scale(full_rows, mlp_gain).astype(jnp.bfloat16)
    logits = jnp.dot(outgoing, router_full, preferred_element_type=jnp.float32)
    residual = lax.dynamic_slice_in_dim(full_rows, tp_place * col_share, col_share, 1)
    expert_ids = jnp.arange(expert_count, dtype=jnp.int32)
    chosen = routes[:, :, None] == expert_ids[None, None, :]
    route_logits = jnp.sum(jnp.where(chosen, logits[:, None, :], 0.0), axis=2)
    route_weight = jax.nn.softmax(route_logits, axis=1) * valid_token[:, None]
    flat_routes = routes.reshape(-1)
    live_route = jnp.repeat(valid_token, route_count)
    one_hot = ((flat_routes[:, None] == expert_ids[None, :]) & live_route[:, None]).astype(
        jnp.int32
    )
    rank_within = jnp.sum((jnp.cumsum(one_hot, axis=0) - one_hot) * one_hot, axis=1)
    slot_index = flat_routes * capacity + rank_within
    target_slot = jnp.where(live_route, slot_index, expert_count * capacity)
    owner_row = jnp.repeat(offsets, route_count) + 1
    source_row = (
        jnp.zeros((expert_count * capacity,), jnp.int32).at[target_slot].set(owner_row, mode="drop")
    )
    buffer = jnp.where(
        (source_row > 0)[:, None],
        outgoing[jnp.maximum(source_row - 1, 0)],
        jnp.zeros((), jnp.bfloat16),
    )
    buffer = buffer.reshape(expert_count, capacity, outgoing.shape[1])
    trainer = jnp.concatenate([expert_gate, expert_up, expert_down], axis=2).astype(jnp.bfloat16)
    ordered = jnp.take(trainer, layout_map, axis=0)
    server = lax.all_to_all(ordered, "seq", split_axis=0, concat_axis=1, tiled=True)
    hidden_share = expert_gate.shape[2]
    local_experts = server.shape[0]
    full_block = lax.all_to_all(buffer, "seq", split_axis=0, concat_axis=0, tiled=True)
    item_count = full_block.shape[1]
    grouped = full_block.reshape(seq_count, local_experts, item_count, model_width)
    gate_up = jnp.einsum(
        "sacd,adf->sacf",
        grouped,
        server[:, :, : 2 * hidden_share],
        preferred_element_type=jnp.float32,
    )
    hidden_state = (jax.nn.silu(gate_up[..., :hidden_share]) * gate_up[..., hidden_share:]).astype(
        jnp.bfloat16
    )
    partial_rows = jnp.einsum(
        "sacf,adf->sacd",
        hidden_state,
        server[:, :, 2 * hidden_share :],
        preferred_element_type=jnp.float32,
    )
    partial_rows = lax.optimization_barrier(partial_rows.astype(jnp.bfloat16)).astype(jnp.float32)
    summed = lax.psum_scatter(
        partial_rows.astype(jnp.bfloat16), "tp", scatter_dimension=3, tiled=True
    )
    returned = lax.all_to_all(
        summed.reshape(seq_count * local_experts, item_count, col_share),
        "seq",
        split_axis=0,
        concat_axis=0,
        tiled=True,
    )
    picked = returned.reshape(expert_count * capacity, col_share)[
        jnp.where(live_route, slot_index, 0)
    ]
    picked = picked.reshape(token_count, route_count, col_share)
    expert_mix = jnp.sum(route_weight[:, :, None] * picked.astype(jnp.float32), axis=1)
    return (residual + expert_mix).astype(jnp.bfloat16)


def solution(mesh):
    placed = (
        P("seq", None),
        P(),
        P(),
        P("seq", "tp"),
        P("seq", "tp"),
        P("seq", "tp"),
        P("tp", "seq"),
        P("tp"),
        P("seq", None),
        P(None, "seq", "tp"),
        P(None, "seq", "tp"),
        P(None, "seq", "tp"),
        P(),
        P(),
        P("seq", None),
    )
    return jax.shard_map(
        shards, mesh=mesh, in_specs=placed, out_specs=P("seq", "tp"), check_vma=False
    )
```

profile of v0, /device:TPU:18, one launch (start us, length us, event | category | flops | bytes accessed | tf_op | source)
XLA Modules:
  0.0 1064.2 jit_solution(7470347210897196199)
XLA Ops:
  35.2 7.2 all-to-all-start
  50.4 233.6 %all-gather.3.cloned.1.call-done = bf16[2048,3072]{1,0:T(8,128)(2,1)} async-done(((bf16[128,3072]{1,0:T(8,128)(2,1)}), bf16[2048,3072]{1,0:T(8,128)(2,1)}) %all-gather.3.cloned.1.call-update) | async-done | bytes 12582928 | tf_op jit(solution)/shard_map/all_gather | solution.py:121
  293.4 493.8 %while.25 = (s32[]{:T(128)}, f32[8,128]{1,0:T(8,128)S(1)}, f32[8,128]{1,0:T(8,128)S(1)}, f32[8,128,128]{2,1,0:T(8,128)S(1)}, bf16[2,128,8,128]{3,1,2,0:T(8,128)(...) while((s32[]{:T(128)}, f32[8,128]{1,0:T(8,128)S(1)}, ...), condition=%wide.region_8.9_spmd.clone, body=%wide.region_4.8_spmd.clone.sunk | while | flops 471806848 | bytes 14038749 | solution.py:162
  300.5 23.3 %collective-permute-done = bf16[2,128,8,128]{3,1,2,0:T(8,128)(2,1)S(1)} collective-permute-done((bf16[2,128,8,128]{3,1,2,0:T(8,128)(2,1)S(1)}, bf16[2,128,8,128]{3,1,2,0:T(8,128)(2,1)S(1)}, u32[]{:S(2)}, u32[]{:S(2)}) %collective-permute-start) | collective-permute-done | bytes 524320 | tf_op jit(solution)/shard_map/while/body/eval_jaxpr/ppermute | solution.py:16
  332.8 20.7 %collective-permute-done = bf16[2,128,8,128]{3,1,2,0:T(8,128)(2,1)S(1)} collective-permute-done((bf16[2,128,8,128]{3,1,2,0:T(8,128)(2,1)S(1)}, bf16[2,128,8,128]{3,1,2,0:T(8,128)(2,1)S(1)}, u32[]{:S(2)}, u32[]{:S(2)}) %collective-permute-start) | collective-permute-done | bytes 524320 | tf_op jit(solution)/shard_map/while/body/eval_jaxpr/ppermute | solution.py:16
  362.5 41.4 %collective-permute-done = bf16[2,128,8,128]{3,1,2,0:T(8,128)(2,1)S(1)} collective-permute-done((bf16[2,128,8,128]{3,1,2,0:T(8,128)(2,1)S(1)}, bf16[2,128,8,128]{3,1,2,0:T(8,128)(2,1)S(1)}, u32[]{:S(2)}, u32[]{:S(2)}) %collective-permute-start) | collective-permute-done | bytes 524320 | tf_op jit(solution)/shard_map/while/body/eval_jaxpr/ppermute | solution.py:16
  413.3 21.1 %collective-permute-done = bf16[2,128,8,128]{3,1,2,0:T(8,128)(2,1)S(1)} collective-permute-done((bf16[2,128,8,128]{3,1,2,0:T(8,128)(2,1)S(1)}, bf16[2,128,8,128]{3,1,2,0:T(8,128)(2,1)S(1)}, u32[]{:S(2)}, u32[]{:S(2)}) %collective-permute-start) | collective-permute-done | bytes 524320 | tf_op jit(solution)/shard_map/while/body/eval_jaxpr/ppermute | solution.py:16
  443.4 19.8 %collective-permute-done = bf16[2,128,8,128]{3,1,2,0:T(8,128)(2,1)S(1)} collective-permute-done((bf16[2,128,8,128]{3,1,2,0:T(8,128)(2,1)S(1)}, bf16[2,128,8,128]{3,1,2,0:T(8,128)(2,1)S(1)}, u32[]{:S(2)}, u32[]{:S(2)}) %collective-permute-start) | collective-permute-done | bytes 524320 | tf_op jit(solution)/shard_map/while/body/eval_jaxpr/ppermute | solution.py:16
  472.2 19.4 %collective-permute-done = bf16[2,128,8,128]{3,1,2,0:T(8,128)(2,1)S(1)} collective-permute-done((bf16[2,128,8,128]{3,1,2,0:T(8,128)(2,1)S(1)}, bf16[2,128,8,128]{3,1,2,0:T(8,128)(2,1)S(1)}, u32[]{:S(2)}, u32[]{:S(2)}) %collective-permute-start) | collective-permute-done | bytes 524320 | tf_op jit(solution)/shard_map/while/body/eval_jaxpr/ppermute | solution.py:16
  500.7 21.3 %collective-permute-done = bf16[2,128,8,128]{3,1,2,0:T(8,128)(2,1)S(1)} collective-permute-done((bf16[2,128,8,128]{3,1,2,0:T(8,128)(2,1)S(1)}, bf16[2,128,8,128]{3,1,2,0:T(8,128)(2,1)S(1)}, u32[]{:S(2)}, u32[]{:S(2)}) %collective-permute-start) | collective-permute-done | bytes 524320 | tf_op jit(solution)/shard_map/while/body/eval_jaxpr/ppermute | solution.py:16
  531.0 19.4 %collective-permute-done = bf16[2,128,8,128]{3,1,2,0:T(8,128)(2,1)S(1)} collective-permute-done((bf16[2,128,8,128]{3,1,2,0:T(8,128)(2,1)S(1)}, bf16[2,128,8,128]{3,1,2,0:T(8,128)(2,1)S(1)}, u32[]{:S(2)}, u32[]{:S(2)}) %collective-permute-start) | collective-permute-done | bytes 524320 | tf_op jit(solution)/shard_map/while/body/eval_jaxpr/ppermute | solution.py:16
  559.4 21.3 %collective-permute-done = bf16[2,128,8,128]{3,1,2,0:T(8,128)(2,1)S(1)} collective-permute-done((bf16[2,128,8,128]{3,1,2,0:T(8,128)(2,1)S(1)}, bf16[2,128,8,128]{3,1,2,0:T(8,128)(2,1)S(1)}, u32[]{:S(2)}, u32[]{:S(2)}) %collective-permute-start) | collective-permute-done | bytes 524320 | tf_op jit(solution)/shard_map/while/body/eval_jaxpr/ppermute | solution.py:16
  589.7 19.4 %collective-permute-done = bf16[2,128,8,128]{3,1,2,0:T(8,128)(2,1)S(1)} collective-permute-done((bf16[2,128,8,128]{3,1,2,0:T(8,128)(2,1)S(1)}, bf16[2,128,8,128]{3,1,2,0:T(8,128)(2,1)S(1)}, u32[]{:S(2)}, u32[]{:S(2)}) %collective-permute-start) | collective-permute-done | bytes 524320 | tf_op jit(solution)/shard_map/while/body/eval_jaxpr/ppermute | solution.py:16
  618.1 21.3 %collective-permute-done = bf16[2,128,8,128]{3,1,2,0:T(8,128)(2,1)S(1)} collective-permute-done((bf16[2,128,8,128]{3,1,2,0:T(8,128)(2,1)S(1)}, bf16[2,128,8,128]{3,1,2,0:T(8,128)(2,1)S(1)}, u32[]{:S(2)}, u32[]{:S(2)}) %collective-permute-start) | collective-permute-done | bytes 524320 | tf_op jit(solution)/shard_map/while/body/eval_jaxpr/ppermute | solution.py:16
  648.4 19.4 %collective-permute-done = bf16[2,128,8,128]{3,1,2,0:T(8,128)(2,1)S(1)} collective-permute-done((bf16[2,128,8,128]{3,1,2,0:T(8,128)(2,1)S(1)}, bf16[2,128,8,128]{3,1,2,0:T(8,128)(2,1)S(1)}, u32[]{:S(2)}, u32[]{:S(2)}) %collective-permute-start) | collective-permute-done | bytes 524320 | tf_op jit(solution)/shard_map/while/body/eval_jaxpr/ppermute | solution.py:16
  676.9 21.3 %collective-permute-done = bf16[2,128,8,128]{3,1,2,0:T(8,128)(2,1)S(1)} collective-permute-done((bf16[2,128,8,128]{3,1,2,0:T(8,128)(2,1)S(1)}, bf16[2,128,8,128]{3,1,2,0:T(8,128)(2,1)S(1)}, u32[]{:S(2)}, u32[]{:S(2)}) %collective-permute-start) | collective-permute-done | bytes 524320 | tf_op jit(solution)/shard_map/while/body/eval_jaxpr/ppermute | solution.py:16
  707.2 19.4 %collective-permute-done = bf16[2,128,8,128]{3,1,2,0:T(8,128)(2,1)S(1)} collective-permute-done((bf16[2,128,8,128]{3,1,2,0:T(8,128)(2,1)S(1)}, bf16[2,128,8,128]{3,1,2,0:T(8,128)(2,1)S(1)}, u32[]{:S(2)}, u32[]{:S(2)}) %collective-permute-start) | collective-permute-done | bytes 524320 | tf_op jit(solution)/shard_map/while/body/eval_jaxpr/ppermute | solution.py:16
  735.6 21.3 %collective-permute-done = bf16[2,128,8,128]{3,1,2,0:T(8,128)(2,1)S(1)} collective-permute-done((bf16[2,128,8,128]{3,1,2,0:T(8,128)(2,1)S(1)}, bf16[2,128,8,128]{3,1,2,0:T(8,128)(2,1)S(1)}, u32[]{:S(2)}, u32[]{:S(2)}) %collective-permute-start) | collective-permute-done | bytes 524320 | tf_op jit(solution)/shard_map/while/body/eval_jaxpr/ppermute | solution.py:16
  765.9 19.4 %collective-permute-done = bf16[2,128,8,128]{3,1,2,0:T(8,128)(2,1)S(1)} collective-permute-done((bf16[2,128,8,128]{3,1,2,0:T(8,128)(2,1)S(1)}, bf16[2,128,8,128]{3,1,2,0:T(8,128)(2,1)S(1)}, u32[]{:S(2)}, u32[]{:S(2)}) %collective-permute-start) | collective-permute-done | bytes 524320 | tf_op jit(solution)/shard_map/while/body/eval_jaxpr/ppermute | solution.py:16
  796.2 15.8 %all-reduce.2.cloned.1.call-done = f32[128,2048]{1,0:T(8,128)} async-done(((f32[128,2048]{1,0:T(8,128)}), f32[128,2048]{1,0:T(8,128)}) %all-reduce.2.cloned.1.call-update) | async-done | bytes 1048592 | tf_op jit(solution)/shard_map/psum | solution.py:176
  825.4 110.3 %all_to_all.22 = bf16[16,72,2048]{2,1,0:T(8,128)(2,1)S(1)} all-to-all(bf16[16,72,2048]{2,1,0:T(8,128)(2,1)} %broadcast_select_fusion.1), channel_id=1, replica_groups=mesh['seq'=16,'tp'=2] {'seq'}, dimensions={0} | all-to-all | bytes 9437184 | tf_op jit(solution)/shard_map/all_to_all | solution.py:208
  935.7 7.3 fusion.14
  949.0 13.0 %reduce-scatter.2.cloned.1.call-done = bf16[16,1,72,1024]{3,2,0,1:T(8,128)(2,1)} async-done(((bf16[16,1,72,2048]{3,2,0,1:T(8,128)(2,1)}), bf16[16,1,72,1024]{3,2,0,1:T(8,128)(2,1)}) %reduce-scatter.2.cloned.1.call-update) | async-done | bytes 2359312 | tf_op jit(solution)/shard_map/reduce_scatter | solution.py:227
  968.9 78.2 %all_gather.11 = bf16[2048,16]{0,1:T(8,128)(2,1)S(1)} all-gather(bf16[128,16]{0,1:T(8,128)(2,1)S(1)} %convert_element_type.94), channel_id=1, replica_groups=mesh['seq'=16,'tp'=2] {'seq'}, dimensions={0}, use_global_device_ids=true | all-gather | bytes 69632 | tf_op jit(solution)/shard_map/all_gather | solution.py:122
  (431 shorter events, 233.7 us)
Async XLA Ops:
  6.5 277.4 %all-gather.3.cloned.1.call-start = ((), (), s32[]{:S(2)}) async-start(), calls=%async_computation.4 | async-start | bytes 13369344 | tf_op jit(solution)/shard_map/all_gather | solution.py:121
  35.2 790.3 %all-to-all-start = ((bf16[16,128,1536]{2,1,0:T(8,128)(2,1)}), bf16[16,128,1536]{2,1,0:T(8,128)(2,1)}, u32[]{:S(2)}, u32[]{:S(2)}) async-start(bf16[16,128,1536]{2,1,0:T(8,128)(2,1)} %broadcast_select_fusion), calls=%async_computation | async-start | bytes 12582912 | tf_op jit(solution)/shard_map/all_to_all | solution.py:205
  42.4 745.1 %all-gather.5.cloned.1.call-start = ((), (), s32[]{:S(2)}) async-start(), calls=%async_computation.5 | async-start | bytes 4456448 | tf_op jit(solution)/shard_map/all_gather | solution.py:173
  43.2 768.7 %all-reduce.2.cloned.1.call-start = ((), (), s32[]{:S(2)}) async-start(), calls=%async_computation.6 | async-start | bytes 2097152 | tf_op jit(solution)/shard_map/psum | solution.py:176
  293.4 30.4 %collective-permute-start.1 = (bf16[2,128,8,128]{3,1,2,0:T(8,128)(2,1)S(1)}, bf16[2,128,8,128]{3,1,2,0:T(8,128)(2,1)S(1)}, u32[]{:S(2)}, u32[]{:S(2)}) collective-permute-start(bf16[2,128,8,128]{3,1,2,0:T(8,128)(2,1)S(1)} %get-tuple-element.428), channel_id=1, source_target_pairs={{2,0},{4,2},{6,4},{8,6},{10,8},{12,10},{14,12},{16,14},{18,16},{20... | collective-permute-start | bytes 1572872 | tf_op jit(solution)/shard_map/while/body/eval_jaxpr/ppermute | solution.py:16
  296.1 27.7 %collective-permute-start = (bf16[2,128,8,128]{3,1,2,0:T(8,128)(2,1)S(1)}, bf16[2,128,8,128]{3,1,2,0:T(8,128)(2,1)S(1)}, u32[]{:S(2)}, u32[]{:S(2)}) collective-permute-start(bf16[2,128,8,128]{3,1,2,0:T(8,128)(2,1)S(1)} %get-tuple-element.427), channel_id=1, source_target_pairs={{0,2},{2,4},{4,6},{6,8},{8,10},{10,12},{12,14},{14,16},{16,18},{18... | collective-permute-start | bytes 1572872 | tf_op jit(solution)/shard_map/while/body/eval_jaxpr/ppermute | solution.py:16
  325.7 27.8 %collective-permute-start.1 = (bf16[2,128,8,128]{3,1,2,0:T(8,128)(2,1)S(1)}, bf16[2,128,8,128]{3,1,2,0:T(8,128)(2,1)S(1)}, u32[]{:S(2)}, u32[]{:S(2)}) collective-permute-start(bf16[2,128,8,128]{3,1,2,0:T(8,128)(2,1)S(1)} %get-tuple-element.428), channel_id=1, source_target_pairs={{2,0},{4,2},{6,4},{8,6},{10,8},{12,10},{14,12},{16,14},{18,16},{20... | collective-permute-start | bytes 1572872 | tf_op jit(solution)/shard_map/while/body/eval_jaxpr/ppermute | solution.py:16
  355.4 48.5 %collective-permute-start.1 = (bf16[2,128,8,128]{3,1,2,0:T(8,128)(2,1)S(1)}, bf16[2,128,8,128]{3,1,2,0:T(8,128)(2,1)S(1)}, u32[]{:S(2)}, u32[]{:S(2)}) collective-permute-start(bf16[2,128,8,128]{3,1,2,0:T(8,128)(2,1)S(1)} %get-tuple-element.428), channel_id=1, source_target_pairs={{2,0},{4,2},{6,4},{8,6},{10,8},{12,10},{14,12},{16,14},{18,16},{20... | collective-permute-start | bytes 1572872 | tf_op jit(solution)/shard_map/while/body/eval_jaxpr/ppermute | solution.py:16
  359.3 44.6 %collective-permute-start = (bf16[2,128,8,128]{3,1,2,0:T(8,128)(2,1)S(1)}, bf16[2,128,8,128]{3,1,2,0:T(8,128)(2,1)S(1)}, u32[]{:S(2)}, u32[]{:S(2)}) collective-permute-start(bf16[2,128,8,128]{3,1,2,0:T(8,128)(2,1)S(1)} %get-tuple-element.427), channel_id=1, source_target_pairs={{0,2},{2,4},{4,6},{6,8},{8,10},{10,12},{12,14},{14,16},{16,18},{18... | collective-permute-start | bytes 1572872 | tf_op jit(solution)/shard_map/while/body/eval_jaxpr/ppermute | solution.py:16
  405.8 28.7 %collective-permute-start.1 = (bf16[2,128,8,128]{3,1,2,0:T(8,128)(2,1)S(1)}, bf16[2,128,8,128]{3,1,2,0:T(8,128)(2,1)S(1)}, u32[]{:S(2)}, u32[]{:S(2)}) collective-permute-start(bf16[2,128,8,128]{3,1,2,0:T(8,128)(2,1)S(1)} %get-tuple-element.428), channel_id=1, source_target_pairs={{2,0},{4,2},{6,4},{8,6},{10,8},{12,10},{14,12},{16,14},{18,16},{20... | collective-permute-start | bytes 1572872 | tf_op jit(solution)/shard_map/while/body/eval_jaxpr/ppermute | solution.py:16
  407.7 26.7 %collective-permute-start = (bf16[2,128,8,128]{3,1,2,0:T(8,128)(2,1)S(1)}, bf16[2,128,8,128]{3,1,2,0:T(8,128)(2,1)S(1)}, u32[]{:S(2)}, u32[]{:S(2)}) collective-permute-start(bf16[2,128,8,128]{3,1,2,0:T(8,128)(2,1)S(1)} %get-tuple-element.427), channel_id=1, source_target_pairs={{0,2},{2,4},{4,6},{6,8},{8,10},{10,12},{12,14},{14,16},{16,18},{18... | collective-permute-start | bytes 1572872 | tf_op jit(solution)/shard_map/while/body/eval_jaxpr/ppermute | solution.py:16
  436.3 27.0 %collective-permute-start.1 = (bf16[2,128,8,128]{3,1,2,0:T(8,128)(2,1)S(1)}, bf16[2,128,8,128]{3,1,2,0:T(8,128)(2,1)S(1)}, u32[]{:S(2)}, u32[]{:S(2)}) collective-permute-start(bf16[2,128,8,128]{3,1,2,0:T(8,128)(2,1)S(1)} %get-tuple-element.428), channel_id=1, source_target_pairs={{2,0},{4,2},{6,4},{8,6},{10,8},{12,10},{14,12},{16,14},{18,16},{20... | collective-permute-start | bytes 1572872 | tf_op jit(solution)/shard_map/while/body/eval_jaxpr/ppermute | solution.py:16
  493.6 28.4 %collective-permute-start.1 = (bf16[2,128,8,128]{3,1,2,0:T(8,128)(2,1)S(1)}, bf16[2,128,8,128]{3,1,2,0:T(8,128)(2,1)S(1)}, u32[]{:S(2)}, u32[]{:S(2)}) collective-permute-start(bf16[2,128,8,128]{3,1,2,0:T(8,128)(2,1)S(1)} %get-tuple-element.428), channel_id=1, source_target_pairs={{2,0},{4,2},{6,4},{8,6},{10,8},{12,10},{14,12},{16,14},{18,16},{20... | collective-permute-start | bytes 1572872 | tf_op jit(solution)/shard_map/while/body/eval_jaxpr/ppermute | solution.py:16
  523.9 26.6 %collective-permute-start.1 = (bf16[2,128,8,128]{3,1,2,0:T(8,128)(2,1)S(1)}, bf16[2,128,8,128]{3,1,2,0:T(8,128)(2,1)S(1)}, u32[]{:S(2)}, u32[]{:S(2)}) collective-permute-start(bf16[2,128,8,128]{3,1,2,0:T(8,128)(2,1)S(1)} %get-tuple-element.428), channel_id=1, source_target_pairs={{2,0},{4,2},{6,4},{8,6},{10,8},{12,10},{14,12},{16,14},{18,16},{20... | collective-permute-start | bytes 1572872 | tf_op jit(solution)/shard_map/while/body/eval_jaxpr/ppermute | solution.py:16
  552.3 28.4 %collective-permute-start.1 = (bf16[2,128,8,128]{3,1,2,0:T(8,128)(2,1)S(1)}, bf16[2,128,8,128]{3,1,2,0:T(8,128)(2,1)S(1)}, u32[]{:S(2)}, u32[]{:S(2)}) collective-permute-start(bf16[2,128,8,128]{3,1,2,0:T(8,128)(2,1)S(1)} %get-tuple-element.428), channel_id=1, source_target_pairs={{2,0},{4,2},{6,4},{8,6},{10,8},{12,10},{14,12},{16,14},{18,16},{20... | collective-permute-start | bytes 1572872 | tf_op jit(solution)/shard_map/while/body/eval_jaxpr/ppermute | solution.py:16
  582.6 26.6 %collective-permute-start.1 = (bf16[2,128,8,128]{3,1,2,0:T(8,128)(2,1)S(1)}, bf16[2,128,8,128]{3,1,2,0:T(8,128)(2,1)S(1)}, u32[]{:S(2)}, u32[]{:S(2)}) collective-permute-start(bf16[2,128,8,128]{3,1,2,0:T(8,128)(2,1)S(1)} %get-tuple-element.428), channel_id=1, source_target_pairs={{2,0},{4,2},{6,4},{8,6},{10,8},{12,10},{14,12},{16,14},{18,16},{20... | collective-permute-start | bytes 1572872 | tf_op jit(solution)/shard_map/while/body/eval_jaxpr/ppermute | solution.py:16
  611.0 28.4 %collective-permute-start.1 = (bf16[2,128,8,128]{3,1,2,0:T(8,128)(2,1)S(1)}, bf16[2,128,8,128]{3,1,2,0:T(8,128)(2,1)S(1)}, u32[]{:S(2)}, u32[]{:S(2)}) collective-permute-start(bf16[2,128,8,128]{3,1,2,0:T(8,128)(2,1)S(1)} %get-tuple-element.428), channel_id=1, source_target_pairs={{2,0},{4,2},{6,4},{8,6},{10,8},{12,10},{14,12},{16,14},{18,16},{20... | collective-permute-start | bytes 1572872 | tf_op jit(solution)/shard_map/while/body/eval_jaxpr/ppermute | solution.py:16
  641.3 26.6 %collective-permute-start.1 = (bf16[2,128,8,128]{3,1,2,0:T(8,128)(2,1)S(1)}, bf16[2,128,8,128]{3,1,2,0:T(8,128)(2,1)S(1)}, u32[]{:S(2)}, u32[]{:S(2)}) collective-permute-start(bf16[2,128,8,128]{3,1,2,0:T(8,128)(2,1)S(1)} %get-tuple-element.428), channel_id=1, source_target_pairs={{2,0},{4,2},{6,4},{8,6},{10,8},{12,10},{14,12},{16,14},{18,16},{20... | collective-permute-start | bytes 1572872 | tf_op jit(solution)/shard_map/while/body/eval_jaxpr/ppermute | solution.py:16
  669.8 28.4 %collective-permute-start.1 = (bf16[2,128,8,128]{3,1,2,0:T(8,128)(2,1)S(1)}, bf16[2,128,8,128]{3,1,2,0:T(8,128)(2,1)S(1)}, u32[]{:S(2)}, u32[]{:S(2)}) collective-permute-start(bf16[2,128,8,128]{3,1,2,0:T(8,128)(2,1)S(1)} %get-tuple-element.428), channel_id=1, source_target_pairs={{2,0},{4,2},{6,4},{8,6},{10,8},{12,10},{14,12},{16,14},{18,16},{20... | collective-permute-start | bytes 1572872 | tf_op jit(solution)/shard_map/while/body/eval_jaxpr/ppermute | solution.py:16
  700.1 26.6 %collective-permute-start.1 = (bf16[2,128,8,128]{3,1,2,0:T(8,128)(2,1)S(1)}, bf16[2,128,8,128]{3,1,2,0:T(8,128)(2,1)S(1)}, u32[]{:S(2)}, u32[]{:S(2)}) collective-permute-start(bf16[2,128,8,128]{3,1,2,0:T(8,128)(2,1)S(1)} %get-tuple-element.428), channel_id=1, source_target_pairs={{2,0},{4,2},{6,4},{8,6},{10,8},{12,10},{14,12},{16,14},{18,16},{20... | collective-permute-start | bytes 1572872 | tf_op jit(solution)/shard_map/while/body/eval_jaxpr/ppermute | solution.py:16
  728.5 28.4 %collective-permute-start.1 = (bf16[2,128,8,128]{3,1,2,0:T(8,128)(2,1)S(1)}, bf16[2,128,8,128]{3,1,2,0:T(8,128)(2,1)S(1)}, u32[]{:S(2)}, u32[]{:S(2)}) collective-permute-start(bf16[2,128,8,128]{3,1,2,0:T(8,128)(2,1)S(1)} %get-tuple-element.428), channel_id=1, source_target_pairs={{2,0},{4,2},{6,4},{8,6},{10,8},{12,10},{14,12},{16,14},{18,16},{20... | collective-permute-start | bytes 1572872 | tf_op jit(solution)/shard_map/while/body/eval_jaxpr/ppermute | solution.py:16
  758.8 26.6 %collective-permute-start.1 = (bf16[2,128,8,128]{3,1,2,0:T(8,128)(2,1)S(1)}, bf16[2,128,8,128]{3,1,2,0:T(8,128)(2,1)S(1)}, u32[]{:S(2)}, u32[]{:S(2)}) collective-permute-start(bf16[2,128,8,128]{3,1,2,0:T(8,128)(2,1)S(1)} %get-tuple-element.428), channel_id=1, source_target_pairs={{2,0},{4,2},{6,4},{8,6},{10,8},{12,10},{14,12},{16,14},{18,16},{20... | collective-permute-start | bytes 1572872 | tf_op jit(solution)/shard_map/while/body/eval_jaxpr/ppermute | solution.py:16
  791.5 170.5 %reduce-scatter.2.cloned.1.call-start = ((), (), s32[]{:S(2)}) async-start(), calls=%async_computation.7 | async-start | bytes 7077888 | tf_op jit(solution)/shard_map/reduce_scatter | solution.py:227
  962.0 85.6 %all-to-all-start.2 = ((bf16[16,72,1024]{2,1,0:T(8,128)(2,1)}), bf16[16,72,1024]{2,1,0:T(8,128)(2,1)S(1)}, u32[]{:S(2)}, u32[]{:S(2)}) async-start(bf16[16,72,1024]{2,1,0:T(8,128)(2,1)} %bitcast.102), calls=%async_computation.3 | async-start | bytes 4718592 | tf_op jit(solution)/shard_map/all_to_all | solution.py:230
  (26 other events, 695.1 us)
Sparse Core Ops, SparseCore 0:
  10.9 272.9 all-gather.2
  286.6 137.9 all-gather.4
  791.6 20.3 all-reduce.1
  949.1 12.8 reduce-scatter.1
where the time goes:
time: 1070 us; the launch traced here: 1060 us
  waiting for transfers between devices  612 us (57%)
  blocking collectives  188 us (18%)
  starting transfers between devices  123 us (11%)
  matrix products  48.1 us (4%)
  other arithmetic  45.3 us (4%)
  local copies, waits for them, and re-layouts  31.9 us (3%)
  between operations  13.6 us (1%)
    ppermute x32, waiting for transfers between devices, from_behind(): lax.ppermute(value, axis, [(source, source + steps) for source in range(f...  349 us
    all_gather x1, waiting for transfers between devices, shards(): stack_piece = lax.all_gather(stack_local, 'seq', axis=0, tiled=True)  234 us
    all_to_all x1, blocking collectives, shards(): lax.all_to_all(buffer, 'seq', split_axis=0, concat_axis=0, tiled=True)  110 us
    ppermute x32, starting transfers between devices, from_behind(): lax.ppermute(value, axis, [(source, source + steps) for source in range(f...  108 us
    all_gather x1, blocking collectives, shards(): router_piece = lax.all_gather(router_local, 'seq', axis=0, tiled=True)  78.2 us
  transfers between devices with their start and end apart: 38, of which 19 were waited for; matrix products, arithmetic and copies ran while one was open for 9% of the time, Pallas kernels for 0%

commit v1 on v0

--- a/solution.py
+++ b/solution.py
@@ -1,3 +1,4 @@
+import functools
 import jax
 import jax.numpy as jnp
 from jax import lax
@@ -8,6 +9,30 @@
 EPSILON = 1e-05
 ROPE_BASE = 50000.0
 MASKED = -1e30
+
+
+def cover_knots(tile_in, peer_axis):
+    vec_out = lax.axis_size(peer_axis)
+    then, right_arr, z_new = (vec_out, lax.axis_index(peer_axis), tile_in.shape[0])
+    y, v_now = (tile_in, 1)
+    while v_now < then:
+        y = jnp.concatenate(
+            [
+                y,
+                lax.ppermute(
+                    y,
+                    axis_name=peer_axis,
+                    perm=list(map(lambda i: (i, (i - v_now) % then), range(then))),
+                ),
+            ],
+            0,
+        )
+        v_now = 2 * v_now
+    val2 = jnp.roll(y, right_arr * z_new, 0)
+    return val2
+
+
+match_plate = functools.partial(cover_knots, peer_axis="seq")
 
 
 def from_behind(value, axis, steps):
@@ -119,7 +144,7 @@
     stack_local = jnp.concatenate([w_query, w_key, w_value], axis=1).astype(jnp.bfloat16)
     router_local = router.astype(jnp.bfloat16)
     stack_piece = lax.all_gather(stack_local, "seq", axis=0, tiled=True)
-    router_piece = lax.all_gather(router_local, "seq", axis=0, tiled=True)
+    router_piece = match_plate(router_local)
     product = jnp.dot(normed, stack_piece, preferred_element_type=jnp.float32)
     router_full = router_piece
     product, router_full = (product, router_full)

time: 1070 us -> 1050 us (0.981)
  blocking collectives: 188 us -> 110 us
  starting transfers between devices: 123 us -> 168 us
  waiting for transfers between devices: 612 us -> 631 us
    all_gather x1 -> x0, blocking collectives: 78.2 us -> none  [shards(): router_piece = lax.all_gather(router_local, 'seq', axis=0, tiled=True)]
    ppermute x0 -> x4, starting transfers between devices: none -> 45.2 us  [cover_knots(): lax.ppermute(y, axis_name=peer_axis, perm=list(map(lambda i: (i, (i - v_n...]
    ppermute x0 -> x4, waiting for transfers between devices: none -> 19.3 us  [cover_knots(): lax.ppermute(y, axis_name=peer_axis, perm=list(map(lambda i: (i, (i - v_n...]
  transfers between devices with their start and end apart: 38 -> 42, of which waited for: 19 -> 23; matrix products, arithmetic and copies ran while one was open for 9% -> 9% of each run, Pallas kernels for 0% -> 0%
where the time goes in v1:
time: 1050 us
  waiting for transfers between devices  631 us (60%)
  starting transfers between devices  168 us (16%)
  blocking collectives  110 us (10%)
  matrix products  48.1 us (5%)
  other arithmetic  45.3 us (4%)
  local copies, waits for them, and re-layouts  32 us (3%)
  between operations  13.6 us (1%)
    ppermute x32, waiting for transfers between devices, from_behind(): lax.ppermute(value, axis, [(source, source + steps) for source in range(f...  350 us
    all_gather x1, waiting for transfers between devices, shards(): stack_piece = lax.all_gather(stack_local, 'seq', axis=0, tiled=True)  234 us
    all_to_all x1, blocking collectives, shards(): lax.all_to_all(buffer, 'seq', split_axis=0, concat_axis=0, tiled=True)  110 us
    ppermute x32, starting transfers between devices, from_behind(): lax.ppermute(value, axis, [(source, source + steps) for source in range(f...  108 us
    ppermute x4, starting transfers between devices, cover_knots(): lax.ppermute(y, axis_name=peer_axis, perm=list(map(lambda i: (i, (i - v_n...  45.2 us
  transfers between devices with their start and end apart: 42, of which 23 were waited for; matrix products, arithmetic and copies ran while one was open for 9% of the time, Pallas kernels for 0%

profile of v1, /device:TPU:18, one launch (start us, length us, event | category | flops | bytes accessed | tf_op | source)
XLA Modules:
  0.0 1050.6 jit_solution(6517056091628822973)
XLA Ops:
  50.4 233.6 %all-gather.3.cloned.1.call-done = bf16[2048,3072]{1,0:T(8,128)(2,1)} async-done(((bf16[128,3072]{1,0:T(8,128)(2,1)}), bf16[2048,3072]{1,0:T(8,128)(2,1)}) %all-gather.3.cloned.1.call-update) | async-done | bytes 12582928 | tf_op jit(solution)/shard_map/all_gather | solution.py:146
  293.4 493.9 %while.25 = (s32[]{:T(128)}, f32[8,128]{1,0:T(8,128)S(1)}, f32[8,128]{1,0:T(8,128)S(1)}, f32[8,128,128]{2,1,0:T(8,128)S(1)}, bf16[2,128,8,128]{3,1,2,0:T(8,128)(...) while((s32[]{:T(128)}, f32[8,128]{1,0:T(8,128)S(1)}, ...), condition=%wide.region_8.9_spmd.clone, body=%wide.region_4.8_spmd.clone.sunk | while | flops 471806848 | bytes 14038749 | solution.py:187
  300.5 23.3 %collective-permute-done = bf16[2,128,8,128]{3,1,2,0:T(8,128)(2,1)S(1)} collective-permute-done((bf16[2,128,8,128]{3,1,2,0:T(8,128)(2,1)S(1)}, bf16[2,128,8,128]{3,1,2,0:T(8,128)(2,1)S(1)}, u32[]{:S(2)}, u32[]{:S(2)}) %collective-permute-start) | collective-permute-done | bytes 524320 | tf_op jit(solution)/shard_map/while/body/eval_jaxpr/ppermute | solution.py:41
  332.8 20.7 %collective-permute-done = bf16[2,128,8,128]{3,1,2,0:T(8,128)(2,1)S(1)} collective-permute-done((bf16[2,128,8,128]{3,1,2,0:T(8,128)(2,1)S(1)}, bf16[2,128,8,128]{3,1,2,0:T(8,128)(2,1)S(1)}, u32[]{:S(2)}, u32[]{:S(2)}) %collective-permute-start) | collective-permute-done | bytes 524320 | tf_op jit(solution)/shard_map/while/body/eval_jaxpr/ppermute | solution.py:41
  362.5 41.4 %collective-permute-done = bf16[2,128,8,128]{3,1,2,0:T(8,128)(2,1)S(1)} collective-permute-done((bf16[2,128,8,128]{3,1,2,0:T(8,128)(2,1)S(1)}, bf16[2,128,8,128]{3,1,2,0:T(8,128)(2,1)S(1)}, u32[]{:S(2)}, u32[]{:S(2)}) %collective-permute-start) | collective-permute-done | bytes 524320 | tf_op jit(solution)/shard_map/while/body/eval_jaxpr/ppermute | solution.py:41
  413.3 21.1 %collective-permute-done = bf16[2,128,8,128]{3,1,2,0:T(8,128)(2,1)S(1)} collective-permute-done((bf16[2,128,8,128]{3,1,2,0:T(8,128)(2,1)S(1)}, bf16[2,128,8,128]{3,1,2,0:T(8,128)(2,1)S(1)}, u32[]{:S(2)}, u32[]{:S(2)}) %collective-permute-start) | collective-permute-done | bytes 524320 | tf_op jit(solution)/shard_map/while/body/eval_jaxpr/ppermute | solution.py:41
  443.5 19.8 %collective-permute-done = bf16[2,128,8,128]{3,1,2,0:T(8,128)(2,1)S(1)} collective-permute-done((bf16[2,128,8,128]{3,1,2,0:T(8,128)(2,1)S(1)}, bf16[2,128,8,128]{3,1,2,0:T(8,128)(2,1)S(1)}, u32[]{:S(2)}, u32[]{:S(2)}) %collective-permute-start) | collective-permute-done | bytes 524320 | tf_op jit(solution)/shard_map/while/body/eval_jaxpr/ppermute | solution.py:41
  472.2 19.5 %collective-permute-done = bf16[2,128,8,128]{3,1,2,0:T(8,128)(2,1)S(1)} collective-permute-done((bf16[2,128,8,128]{3,1,2,0:T(8,128)(2,1)S(1)}, bf16[2,128,8,128]{3,1,2,0:T(8,128)(2,1)S(1)}, u32[]{:S(2)}, u32[]{:S(2)}) %collective-permute-start) | collective-permute-done | bytes 524320 | tf_op jit(solution)/shard_map/while/body/eval_jaxpr/ppermute | solution.py:41
  500.7 21.2 %collective-permute-done = bf16[2,128,8,128]{3,1,2,0:T(8,128)(2,1)S(1)} collective-permute-done((bf16[2,128,8,128]{3,1,2,0:T(8,128)(2,1)S(1)}, bf16[2,128,8,128]{3,1,2,0:T(8,128)(2,1)S(1)}, u32[]{:S(2)}, u32[]{:S(2)}) %collective-permute-start) | collective-permute-done | bytes 524320 | tf_op jit(solution)/shard_map/while/body/eval_jaxpr/ppermute | solution.py:41
  530.9 19.5 %collective-permute-done = bf16[2,128,8,128]{3,1,2,0:T(8,128)(2,1)S(1)} collective-permute-done((bf16[2,128,8,128]{3,1,2,0:T(8,128)(2,1)S(1)}, bf16[2,128,8,128]{3,1,2,0:T(8,128)(2,1)S(1)}, u32[]{:S(2)}, u32[]{:S(2)}) %collective-permute-start) | collective-permute-done | bytes 524320 | tf_op jit(solution)/shard_map/while/body/eval_jaxpr/ppermute | solution.py:41
  559.5 21.2 %collective-permute-done = bf16[2,128,8,128]{3,1,2,0:T(8,128)(2,1)S(1)} collective-permute-done((bf16[2,128,8,128]{3,1,2,0:T(8,128)(2,1)S(1)}, bf16[2,128,8,128]{3,1,2,0:T(8,128)(2,1)S(1)}, u32[]{:S(2)}, u32[]{:S(2)}) %collective-permute-start) | collective-permute-done | bytes 524320 | tf_op jit(solution)/shard_map/while/body/eval_jaxpr/ppermute | solution.py:41
  589.7 19.5 %collective-permute-done = bf16[2,128,8,128]{3,1,2,0:T(8,128)(2,1)S(1)} collective-permute-done((bf16[2,128,8,128]{3,1,2,0:T(8,128)(2,1)S(1)}, bf16[2,128,8,128]{3,1,2,0:T(8,128)(2,1)S(1)}, u32[]{:S(2)}, u32[]{:S(2)}) %collective-permute-start) | collective-permute-done | bytes 524320 | tf_op jit(solution)/shard_map/while/body/eval_jaxpr/ppermute | solution.py:41
  618.2 21.2 %collective-permute-done = bf16[2,128,8,128]{3,1,2,0:T(8,128)(2,1)S(1)} collective-permute-done((bf16[2,128,8,128]{3,1,2,0:T(8,128)(2,1)S(1)}, bf16[2,128,8,128]{3,1,2,0:T(8,128)(2,1)S(1)}, u32[]{:S(2)}, u32[]{:S(2)}) %collective-permute-start) | collective-permute-done | bytes 524320 | tf_op jit(solution)/shard_map/while/body/eval_jaxpr/ppermute | solution.py:41
  648.4 19.5 %collective-permute-done = bf16[2,128,8,128]{3,1,2,0:T(8,128)(2,1)S(1)} collective-permute-done((bf16[2,128,8,128]{3,1,2,0:T(8,128)(2,1)S(1)}, bf16[2,128,8,128]{3,1,2,0:T(8,128)(2,1)S(1)}, u32[]{:S(2)}, u32[]{:S(2)}) %collective-permute-start) | collective-permute-done | bytes 524320 | tf_op jit(solution)/shard_map/while/body/eval_jaxpr/ppermute | solution.py:41
  676.9 21.2 %collective-permute-done = bf16[2,128,8,128]{3,1,2,0:T(8,128)(2,1)S(1)} collective-permute-done((bf16[2,128,8,128]{3,1,2,0:T(8,128)(2,1)S(1)}, bf16[2,128,8,128]{3,1,2,0:T(8,128)(2,1)S(1)}, u32[]{:S(2)}, u32[]{:S(2)}) %collective-permute-start) | collective-permute-done | bytes 524320 | tf_op jit(solution)/shard_map/while/body/eval_jaxpr/ppermute | solution.py:41
  707.1 19.5 %collective-permute-done = bf16[2,128,8,128]{3,1,2,0:T(8,128)(2,1)S(1)} collective-permute-done((bf16[2,128,8,128]{3,1,2,0:T(8,128)(2,1)S(1)}, bf16[2,128,8,128]{3,1,2,0:T(8,128)(2,1)S(1)}, u32[]{:S(2)}, u32[]{:S(2)}) %collective-permute-start) | collective-permute-done | bytes 524320 | tf_op jit(solution)/shard_map/while/body/eval_jaxpr/ppermute | solution.py:41
  735.7 21.2 %collective-permute-done = bf16[2,128,8,128]{3,1,2,0:T(8,128)(2,1)S(1)} collective-permute-done((bf16[2,128,8,128]{3,1,2,0:T(8,128)(2,1)S(1)}, bf16[2,128,8,128]{3,1,2,0:T(8,128)(2,1)S(1)}, u32[]{:S(2)}, u32[]{:S(2)}) %collective-permute-start) | collective-permute-done | bytes 524320 | tf_op jit(solution)/shard_map/while/body/eval_jaxpr/ppermute | solution.py:41
  765.9 19.5 %collective-permute-done = bf16[2,128,8,128]{3,1,2,0:T(8,128)(2,1)S(1)} collective-permute-done((bf16[2,128,8,128]{3,1,2,0:T(8,128)(2,1)S(1)}, bf16[2,128,8,128]{3,1,2,0:T(8,128)(2,1)S(1)}, u32[]{:S(2)}, u32[]{:S(2)}) %collective-permute-start) | collective-permute-done | bytes 524320 | tf_op jit(solution)/shard_map/while/body/eval_jaxpr/ppermute | solution.py:41
  796.2 15.7 %all-reduce.2.cloned.1.call-done = f32[128,2048]{1,0:T(8,128)} async-done(((f32[128,2048]{1,0:T(8,128)}), f32[128,2048]{1,0:T(8,128)}) %all-reduce.2.cloned.1.call-update) | async-done | bytes 1048592 | tf_op jit(solution)/shard_map/psum | solution.py:201
  825.4 110.3 %all_to_all.22 = bf16[16,72,2048]{2,1,0:T(8,128)(2,1)S(1)} all-to-all(bf16[16,72,2048]{2,1,0:T(8,128)(2,1)} %broadcast_select_fusion.1), channel_id=1, replica_groups=mesh['seq'=16,'tp'=2] {'seq'}, dimensions={0} | all-to-all | bytes 9437184 | tf_op jit(solution)/shard_map/all_to_all | solution.py:233
  935.7 7.3 fusion.14
  949.0 13.0 %reduce-scatter.2.cloned.1.call-done = bf16[16,1,72,1024]{3,2,0,1:T(8,128)(2,1)} async-done(((bf16[16,1,72,2048]{3,2,0,1:T(8,128)(2,1)}), bf16[16,1,72,1024]{3,2,0,1:T(8,128)(2,1)}) %reduce-scatter.2.cloned.1.call-update) | async-done | bytes 2359312 | tf_op jit(solution)/shard_map/reduce_scatter | solution.py:252
  969.5 10.4 collective-permute-done.2
  979.9 43.5 %collective-permute-start.3 = (bf16[256,16]{0,1:T(8,128)(2,1)S(1)}, bf16[256,16]{0,1:T(8,128)(2,1)S(1)}, u32[]{:S(2)}, u32[]{:S(2)}) collective-permute-start(bf16[256,16]{0,1:T(8,128)(2,1)S(1)} %pad_maximum_fusion.6), channel_id=1, source_target_pairs={{0,28},{2,30},{4,0},{6,2},{8,4},{10,6},{12,8},{14,10},{16,12},{18,... | collective-permute-start | bytes 24584 | tf_op jit(solution)/shard_map/ppermute | solution.py:22
  (450 shorter events, 251.5 us)
Async XLA Ops:
  6.5 277.4 %all-gather.3.cloned.1.call-start = ((), (), s32[]{:S(2)}) async-start(), calls=%async_computation.4 | async-start | bytes 13369344 | tf_op jit(solution)/shard_map/all_gather | solution.py:146
  35.2 790.2 %all-to-all-start = ((bf16[16,128,1536]{2,1,0:T(8,128)(2,1)}), bf16[16,128,1536]{2,1,0:T(8,128)(2,1)}, u32[]{:S(2)}, u32[]{:S(2)}) async-start(bf16[16,128,1536]{2,1,0:T(8,128)(2,1)} %broadcast_select_fusion), calls=%async_computation | async-start | bytes 12582912 | tf_op jit(solution)/shard_map/all_to_all | solution.py:230
  42.4 745.2 %all-gather.5.cloned.1.call-start = ((), (), s32[]{:S(2)}) async-start(), calls=%async_computation.5 | async-start | bytes 4456448 | tf_op jit(solution)/shard_map/all_gather | solution.py:198
  43.2 768.7 %all-reduce.2.cloned.1.call-start = ((), (), s32[]{:S(2)}) async-start(), calls=%async_computation.6 | async-start | bytes 2097152 | tf_op jit(solution)/shard_map/psum | solution.py:201
  293.4 30.4 %collective-permute-start.1 = (bf16[2,128,8,128]{3,1,2,0:T(8,128)(2,1)S(1)}, bf16[2,128,8,128]{3,1,2,0:T(8,128)(2,1)S(1)}, u32[]{:S(2)}, u32[]{:S(2)}) collective-permute-start(bf16[2,128,8,128]{3,1,2,0:T(8,128)(2,1)S(1)} %get-tuple-element.430), channel_id=1, source_target_pairs={{2,0},{4,2},{6,4},{8,6},{10,8},{12,10},{14,12},{16,14},{18,16},{20... | collective-permute-start | bytes 1572872 | tf_op jit(solution)/shard_map/while/body/eval_jaxpr/ppermute | solution.py:41
  296.1 27.7 %collective-permute-start = (bf16[2,128,8,128]{3,1,2,0:T(8,128)(2,1)S(1)}, bf16[2,128,8,128]{3,1,2,0:T(8,128)(2,1)S(1)}, u32[]{:S(2)}, u32[]{:S(2)}) collective-permute-start(bf16[2,128,8,128]{3,1,2,0:T(8,128)(2,1)S(1)} %get-tuple-element.429), channel_id=1, source_target_pairs={{0,2},{2,4},{4,6},{6,8},{8,10},{10,12},{12,14},{14,16},{16,18},{18... | collective-permute-start | bytes 1572872 | tf_op jit(solution)/shard_map/while/body/eval_jaxpr/ppermute | solution.py:41
  325.7 27.8 %collective-permute-start.1 = (bf16[2,128,8,128]{3,1,2,0:T(8,128)(2,1)S(1)}, bf16[2,128,8,128]{3,1,2,0:T(8,128)(2,1)S(1)}, u32[]{:S(2)}, u32[]{:S(2)}) collective-permute-start(bf16[2,128,8,128]{3,1,2,0:T(8,128)(2,1)S(1)} %get-tuple-element.430), channel_id=1, source_target_pairs={{2,0},{4,2},{6,4},{8,6},{10,8},{12,10},{14,12},{16,14},{18,16},{20... | collective-permute-start | bytes 1572872 | tf_op jit(solution)/shard_map/while/body/eval_jaxpr/ppermute | solution.py:41
  355.4 48.5 %collective-permute-start.1 = (bf16[2,128,8,128]{3,1,2,0:T(8,128)(2,1)S(1)}, bf16[2,128,8,128]{3,1,2,0:T(8,128)(2,1)S(1)}, u32[]{:S(2)}, u32[]{:S(2)}) collective-permute-start(bf16[2,128,8,128]{3,1,2,0:T(8,128)(2,1)S(1)} %get-tuple-element.430), channel_id=1, source_target_pairs={{2,0},{4,2},{6,4},{8,6},{10,8},{12,10},{14,12},{16,14},{18,16},{20... | collective-permute-start | bytes 1572872 | tf_op jit(solution)/shard_map/while/body/eval_jaxpr/ppermute | solution.py:41
  359.2 44.6 %collective-permute-start = (bf16[2,128,8,128]{3,1,2,0:T(8,128)(2,1)S(1)}, bf16[2,128,8,128]{3,1,2,0:T(8,128)(2,1)S(1)}, u32[]{:S(2)}, u32[]{:S(2)}) collective-permute-start(bf16[2,128,8,128]{3,1,2,0:T(8,128)(2,1)S(1)} %get-tuple-element.429), channel_id=1, source_target_pairs={{0,2},{2,4},{4,6},{6,8},{8,10},{10,12},{12,14},{14,16},{16,18},{18... | collective-permute-start | bytes 1572872 | tf_op jit(solution)/shard_map/while/body/eval_jaxpr/ppermute | solution.py:41
  405.8 28.7 %collective-permute-start.1 = (bf16[2,128,8,128]{3,1,2,0:T(8,128)(2,1)S(1)}, bf16[2,128,8,128]{3,1,2,0:T(8,128)(2,1)S(1)}, u32[]{:S(2)}, u32[]{:S(2)}) collective-permute-start(bf16[2,128,8,128]{3,1,2,0:T(8,128)(2,1)S(1)} %get-tuple-element.430), channel_id=1, source_target_pairs={{2,0},{4,2},{6,4},{8,6},{10,8},{12,10},{14,12},{16,14},{18,16},{20... | collective-permute-start | bytes 1572872 | tf_op jit(solution)/shard_map/while/body/eval_jaxpr/ppermute | solution.py:41
  407.7 26.8 %collective-permute-start = (bf16[2,128,8,128]{3,1,2,0:T(8,128)(2,1)S(1)}, bf16[2,128,8,128]{3,1,2,0:T(8,128)(2,1)S(1)}, u32[]{:S(2)}, u32[]{:S(2)}) collective-permute-start(bf16[2,128,8,128]{3,1,2,0:T(8,128)(2,1)S(1)} %get-tuple-element.429), channel_id=1, source_target_pairs={{0,2},{2,4},{4,6},{6,8},{8,10},{10,12},{12,14},{14,16},{16,18},{18... | collective-permute-start | bytes 1572872 | tf_op jit(solution)/shard_map/while/body/eval_jaxpr/ppermute | solution.py:41
  436.4 26.9 %collective-permute-start.1 = (bf16[2,128,8,128]{3,1,2,0:T(8,128)(2,1)S(1)}, bf16[2,128,8,128]{3,1,2,0:T(8,128)(2,1)S(1)}, u32[]{:S(2)}, u32[]{:S(2)}) collective-permute-start(bf16[2,128,8,128]{3,1,2,0:T(8,128)(2,1)S(1)} %get-tuple-element.430), channel_id=1, source_target_pairs={{2,0},{4,2},{6,4},{8,6},{10,8},{12,10},{14,12},{16,14},{18,16},{20... | collective-permute-start | bytes 1572872 | tf_op jit(solution)/shard_map/while/body/eval_jaxpr/ppermute | solution.py:41
  493.6 28.3 %collective-permute-start.1 = (bf16[2,128,8,128]{3,1,2,0:T(8,128)(2,1)S(1)}, bf16[2,128,8,128]{3,1,2,0:T(8,128)(2,1)S(1)}, u32[]{:S(2)}, u32[]{:S(2)}) collective-permute-start(bf16[2,128,8,128]{3,1,2,0:T(8,128)(2,1)S(1)} %get-tuple-element.430), channel_id=1, source_target_pairs={{2,0},{4,2},{6,4},{8,6},{10,8},{12,10},{14,12},{16,14},{18,16},{20... | collective-permute-start | bytes 1572872 | tf_op jit(solution)/shard_map/while/body/eval_jaxpr/ppermute | solution.py:41
  552.4 28.3 %collective-permute-start.1 = (bf16[2,128,8,128]{3,1,2,0:T(8,128)(2,1)S(1)}, bf16[2,128,8,128]{3,1,2,0:T(8,128)(2,1)S(1)}, u32[]{:S(2)}, u32[]{:S(2)}) collective-permute-start(bf16[2,128,8,128]{3,1,2,0:T(8,128)(2,1)S(1)} %get-tuple-element.430), channel_id=1, source_target_pairs={{2,0},{4,2},{6,4},{8,6},{10,8},{12,10},{14,12},{16,14},{18,16},{20... | collective-permute-start | bytes 1572872 | tf_op jit(solution)/shard_map/while/body/eval_jaxpr/ppermute | solution.py:41
  582.6 26.7 %collective-permute-start.1 = (bf16[2,128,8,128]{3,1,2,0:T(8,128)(2,1)S(1)}, bf16[2,128,8,128]{3,1,2,0:T(8,128)(2,1)S(1)}, u32[]{:S(2)}, u32[]{:S(2)}) collective-permute-start(bf16[2,128,8,128]{3,1,2,0:T(8,128)(2,1)S(1)} %get-tuple-element.430), channel_id=1, source_target_pairs={{2,0},{4,2},{6,4},{8,6},{10,8},{12,10},{14,12},{16,14},{18,16},{20... | collective-permute-start | bytes 1572872 | tf_op jit(solution)/shard_map/while/body/eval_jaxpr/ppermute | solution.py:41
  611.1 28.3 %collective-permute-start.1 = (bf16[2,128,8,128]{3,1,2,0:T(8,128)(2,1)S(1)}, bf16[2,128,8,128]{3,1,2,0:T(8,128)(2,1)S(1)}, u32[]{:S(2)}, u32[]{:S(2)}) collective-permute-start(bf16[2,128,8,128]{3,1,2,0:T(8,128)(2,1)S(1)} %get-tuple-element.430), channel_id=1, source_target_pairs={{2,0},{4,2},{6,4},{8,6},{10,8},{12,10},{14,12},{16,14},{18,16},{20... | collective-permute-start | bytes 1572872 | tf_op jit(solution)/shard_map/while/body/eval_jaxpr/ppermute | solution.py:41
  641.3 26.7 %collective-permute-start.1 = (bf16[2,128,8,128]{3,1,2,0:T(8,128)(2,1)S(1)}, bf16[2,128,8,128]{3,1,2,0:T(8,128)(2,1)S(1)}, u32[]{:S(2)}, u32[]{:S(2)}) collective-permute-start(bf16[2,128,8,128]{3,1,2,0:T(8,128)(2,1)S(1)} %get-tuple-element.430), channel_id=1, source_target_pairs={{2,0},{4,2},{6,4},{8,6},{10,8},{12,10},{14,12},{16,14},{18,16},{20... | collective-permute-start | bytes 1572872 | tf_op jit(solution)/shard_map/while/body/eval_jaxpr/ppermute | solution.py:41
  669.9 28.3 %collective-permute-start.1 = (bf16[2,128,8,128]{3,1,2,0:T(8,128)(2,1)S(1)}, bf16[2,128,8,128]{3,1,2,0:T(8,128)(2,1)S(1)}, u32[]{:S(2)}, u32[]{:S(2)}) collective-permute-start(bf16[2,128,8,128]{3,1,2,0:T(8,128)(2,1)S(1)} %get-tuple-element.430), channel_id=1, source_target_pairs={{2,0},{4,2},{6,4},{8,6},{10,8},{12,10},{14,12},{16,14},{18,16},{20... | collective-permute-start | bytes 1572872 | tf_op jit(solution)/shard_map/while/body/eval_jaxpr/ppermute | solution.py:41
  700.1 26.7 %collective-permute-start.1 = (bf16[2,128,8,128]{3,1,2,0:T(8,128)(2,1)S(1)}, bf16[2,128,8,128]{3,1,2,0:T(8,128)(2,1)S(1)}, u32[]{:S(2)}, u32[]{:S(2)}) collective-permute-start(bf16[2,128,8,128]{3,1,2,0:T(8,128)(2,1)S(1)} %get-tuple-element.430), channel_id=1, source_target_pairs={{2,0},{4,2},{6,4},{8,6},{10,8},{12,10},{14,12},{16,14},{18,16},{20... | collective-permute-start | bytes 1572872 | tf_op jit(solution)/shard_map/while/body/eval_jaxpr/ppermute | solution.py:41
  728.6 28.3 %collective-permute-start.1 = (bf16[2,128,8,128]{3,1,2,0:T(8,128)(2,1)S(1)}, bf16[2,128,8,128]{3,1,2,0:T(8,128)(2,1)S(1)}, u32[]{:S(2)}, u32[]{:S(2)}) collective-permute-start(bf16[2,128,8,128]{3,1,2,0:T(8,128)(2,1)S(1)} %get-tuple-element.430), channel_id=1, source_target_pairs={{2,0},{4,2},{6,4},{8,6},{10,8},{12,10},{14,12},{16,14},{18,16},{20... | collective-permute-start | bytes 1572872 | tf_op jit(solution)/shard_map/while/body/eval_jaxpr/ppermute | solution.py:41
  758.8 26.7 %collective-permute-start.1 = (bf16[2,128,8,128]{3,1,2,0:T(8,128)(2,1)S(1)}, bf16[2,128,8,128]{3,1,2,0:T(8,128)(2,1)S(1)}, u32[]{:S(2)}, u32[]{:S(2)}) collective-permute-start(bf16[2,128,8,128]{3,1,2,0:T(8,128)(2,1)S(1)} %get-tuple-element.430), channel_id=1, source_target_pairs={{2,0},{4,2},{6,4},{8,6},{10,8},{12,10},{14,12},{16,14},{18,16},{20... | collective-permute-start | bytes 1572872 | tf_op jit(solution)/shard_map/while/body/eval_jaxpr/ppermute | solution.py:41
  791.6 170.4 %reduce-scatter.2.cloned.1.call-start = ((), (), s32[]{:S(2)}) async-start(), calls=%async_computation.7 | async-start | bytes 7077888 | tf_op jit(solution)/shard_map/reduce_scatter | solution.py:252
  961.9 72.0 %all-to-all-start.2 = ((bf16[16,72,1024]{2,1,0:T(8,128)(2,1)}), bf16[16,72,1024]{2,1,0:T(8,128)(2,1)S(1)}, u32[]{:S(2)}, u32[]{:S(2)}) async-start(bf16[16,72,1024]{2,1,0:T(8,128)(2,1)} %bitcast.101), calls=%async_computation.3 | async-start | bytes 4718592 | tf_op jit(solution)/shard_map/all_to_all | solution.py:255
  979.9 44.9 %collective-permute-start.3 = (bf16[256,16]{0,1:T(8,128)(2,1)S(1)}, bf16[256,16]{0,1:T(8,128)(2,1)S(1)}, u32[]{:S(2)}, u32[]{:S(2)}) collective-permute-start(bf16[256,16]{0,1:T(8,128)(2,1)S(1)} %pad_maximum_fusion.6), channel_id=1, source_target_pairs={{0,28},{2,30},{4,0},{6,2},{8,4},{10,6},{12,8},{14,10},{16,12},{18,... | collective-permute-start | bytes 24584 | tf_op jit(solution)/shard_map/ppermute | solution.py:22
  (30 other events, 741.4 us)
Sparse Core Ops, SparseCore 0:
  10.9 273.0 all-gather.2
  286.6 137.9 all-gather.4
  791.7 20.2 all-reduce.1
  949.1 12.8 reduce-scatter.1
